TPU v7x, 512 devices: a whole 4x4x16 slice. The times are simulated.
512 devices in a mesh: tm: 16 (over x, z_hi), tmpl: 32 (over y, z_lo, core).
Axes of the slice: x: 4, y: 4, z: 16 (z_hi: 4, z_lo: 4; z = z_hi * 4 + z_lo), core: 2. Of those that a mesh axis runs over, the one named last changes fastest.
Arguments:
- seismic: bfloat16 [512, 3, 16384], P(('tmpl', 'tm')), may hold values from -6 to 6
- templates: bfloat16 [512, 32, 3, 256], P(('tmpl', 'tm')), may hold values from -0.009765625 to 0.009765625
- moveout: int32 [512, 32], P('tmpl'), may hold values from 0 to 128
- active: int32 [512], P('tmpl'), may hold values 0 or 1
Outputs:
- stack: float32 [32, 16384], P('tmpl', 'tm')
All inputs are finite; a program needn't handle non-finite values. No bound on the sum of `active` on one device may be relied on, other than what follows from the above.
Results may differ from a plain program's by a relative error of at most 0.0052.
Values may be sent and summed in bfloat16 or wider, within the bound.
A program may use at most 64 MiB of HBM per device.

v0:
```python
import math

import jax
import jax.numpy as jnp
from jax import lax
from jax.sharding import PartitionSpec as P

L = 256
NF = 512
BLK = 128
TPL = 32


def shifted(block, axis, distance):
    devices = range(lax.axis_size(axis))
    route = [(i - distance, i) for i in devices if i - distance in devices]
    return lax.ppermute(block, axis, route)


def forward_table(count, size):
    sample = jnp.arange(count, dtype=jnp.int32)[:, None]
    freq = jnp.arange(size, dtype=jnp.int32)[None, :]
    angle = 2.0 * math.pi / size * (sample * freq % size).astype(jnp.float32)
    return jnp.concatenate([jnp.cos(angle), -jnp.sin(angle)], axis=1).astype(jnp.bfloat16)


def inverse_table(size, outputs):
    freq = jnp.arange(size, dtype=jnp.int32)[:, None]
    lag = jnp.arange(outputs, dtype=jnp.int32)[None, :]
    angle = 2.0 * math.pi / size * (freq * lag % size).astype(jnp.float32)
    return jnp.concatenate([jnp.cos(angle), -jnp.sin(angle)], axis=0) / size


def framed(signal, blocks):
    leading = signal.shape[:-1]
    pieces = signal.reshape(leading + (signal.shape[-1] // BLK, BLK))
    return jnp.concatenate(
        [pieces[..., offset : offset + blocks, :] for offset in range(NF // BLK)], axis=-1
    )


def station_spectrum(wave, shift_row, active_flag, table, size):
    count_tmpl, chans, length = wave.shape
    spectrum = jnp.dot(
        wave.reshape(count_tmpl * chans, length), table, preferred_element_type=jnp.float32
    )
    spectrum = spectrum.reshape(count_tmpl, chans, 2 * size)
    real_part = spectrum[..., :size]
    imag_part = spectrum[..., size:]
    freq = jnp.arange(size, dtype=jnp.int32)[None, :]
    angle = 2.0 * math.pi / size * (shift_row[:, None] * freq % size).astype(jnp.float32)
    cosine = jnp.cos(angle)[:, None, :]
    sine = jnp.sin(angle)[:, None, :]
    weight = active_flag.astype(jnp.float32)
    out_real = (real_part * cosine + imag_part * sine) * weight
    out_imag = (real_part * sine - imag_part * cosine) * weight
    return jnp.concatenate([out_real, out_imag], axis=-1).astype(jnp.bfloat16)


def accumulate(weighted, spectra):
    x_real = spectra[..., :NF]
    x_imag = spectra[..., NF:]
    g_real = weighted[..., :NF]
    g_imag = weighted[..., NF:]
    total_real = jnp.einsum(
        "stcf,scnf->tnf", g_real, x_real, preferred_element_type=jnp.float32
    ) - jnp.einsum("stcf,scnf->tnf", g_imag, x_imag, preferred_element_type=jnp.float32)
    total_imag = jnp.einsum(
        "stcf,scnf->tnf", g_real, x_imag, preferred_element_type=jnp.float32
    ) + jnp.einsum("stcf,scnf->tnf", g_imag, x_real, preferred_element_type=jnp.float32)
    return (total_real, total_imag)


def per_device(seismic, templates, moveout, active):
    tm_count = lax.axis_size("tm")
    chans = seismic.shape[1]
    window = seismic.shape[2]
    segment = window // tm_count
    margin = NF - BLK
    tmpl_table = forward_table(L, NF)
    data_table = forward_table(NF, NF)
    backward = inverse_table(NF, BLK)

    def one_station(entry):
        return station_spectrum(entry[0], entry[1], entry[2], tmpl_table, NF)

    blocks = segment // BLK
    regrouped = lax.all_to_all(seismic, "tm", split_axis=2, concat_axis=0, tiled=True)
    following = shifted(regrouped[:, :, :margin], "tm", -1)
    extended = jnp.concatenate([regrouped, following], axis=2)
    group_size = extended.shape[0]
    frames = framed(extended, blocks)
    data_spectrum = jnp.dot(
        frames.reshape(group_size * chans * blocks, NF),
        data_table,
        preferred_element_type=jnp.float32,
    )
    data_spectrum = data_spectrum.astype(jnp.bfloat16).reshape(group_size, chans, blocks, 2 * NF)
    weighted = lax.map(
        one_station, (lax.all_gather(templates, "tm", axis=0, tiled=True), moveout, active)
    )
    totals = accumulate(weighted, data_spectrum)
    combined = jnp.concatenate([totals[0], totals[1]], axis=-1)
    series = jnp.dot(
        combined.reshape(TPL // lax.axis_size("tmpl") * lax.axis_size("tmpl") * blocks, 2 * NF),
        backward,
        precision=lax.Precision.HIGHEST,
        preferred_element_type=jnp.float32,
    )
    return lax.psum_scatter(
        series.reshape(TPL // lax.axis_size("tmpl") * lax.axis_size("tmpl"), segment),
        "tmpl",
        scatter_dimension=0,
        tiled=True,
    )


def solution(mesh):
    in_specs = (
        P(("tmpl", "tm"), None, None),
        P(("tmpl", "tm"), None, None, None),
        P("tmpl", None),
        P("tmpl"),
    )
    out_specs = P("tmpl", "tm")
    return jax.shard_map(
        per_device, mesh=mesh, in_specs=in_specs, out_specs=out_specs, check_vma=False
    )
```

profile of v0, /device:TPU:1, one launch (start us, length us, event | category | flops | bytes accessed | tf_op | source)
XLA Modules:
  0.0 625.7 jit_solution(12193715638436342106)
XLA Ops:
  6.5 15.3 %copy.24 = bf16[1,3,16384]{1,0,2:T(2,128)(2,1)} copy(bf16[1,3,16384]{2,1,0:T(4,128)(2,1)} %param.6) | data formatting | bytes 196608 | tf_op args[0]
  22.4 90.8 %reduce = bf16[16384,3]{1,0:T(8,128)(2,1)} reduce(bf16[16384,1,3]{2,1,0:T(2,128)(2,1)} %bitcast.71, bf16[]{:T(256)} %broadcast.142), dimensions={1}, to_apply=%bitcast.50.reduce_sub_computation | reduce | bytes 196610
  113.1 7.5 %reshape.126 = bf16[16,2,1536]{2,1,0:T(2,128)(2,1)} reshape(bf16[16384,3]{1,0:T(8,128)(2,1)} %reduce) | data formatting | bytes 196608
  120.6 18.2 %all-to-all-start = ((bf16[16,2,1536]{2,1,0:T(2,128)(2,1)}), bf16[16,2,1536]{2,1,0:T(2,128)(2,1)S(1)}, u32[]{:S(2)}, u32[]{:S(2)}) async-start(bf16[16,2,1536]{2,1,0:T(2,128)(2,1)} %reshape.126), calls=%async_computation | async-start | bytes 196608 | tf_op jit(solution)/shard_map/all_to_all | solution.py:88
  138.8 2.2 negate_convert_fusion.1
  141.0 64.9 %all_gather.3 = bf16[16,32,3,256]{3,1,2,0:T(8,128)(2,1)S(1)} all-gather(bf16[1,32,3,256]{3,1,2,0:T(8,128)(2,1)S(1)} %copy-done.3), channel_id=1, replica_groups=mesh['tm'=16,'tmpl'=32] {'tm'}, dimensions={0}, use_global_device_ids=true | all-gather | bytes 835584 | tf_op jit(solution)/shard_map/all_gather | solution.py:100
  206.0 54.6 %while.12 = (s32[]{:T(128)}, bf16[16,32,3,1024]{3,1,2,0:T(8,128)(2,1)}, bf16[16,32,3,256]{3,1,2,0:T(8,128)(2,1)S(1)}, bf16[256,1024]{1,0:T(8,128)(2,1)S(1)}, s32[16,32]{1,0:T(8,128)}, /*index=5*/s32[16]{0:T(128)S(1)}, s32[]{:T(128)}) while((s32[]{:T(128)}, bf16[16,32,3,1024]{3,1,2,0:T(8,128)(2,1)}, bf16[16,32,3,256]{3,1,2,0:T(8,128)(2,1)S(1)}, ...), condition=%wide.region_1.2_spmd, body=%wide.region_0.1_spmd.sunk | while | flops 51445760 | bytes 2212845 | solution.py:99
  206.2 0.7 fusion.77
  209.6 0.7 fusion.77
  212.1 0.7 maximum_dynamic-update-slice_fusion.2
  213.1 0.7 fusion.77
  215.6 0.7 maximum_dynamic-update-slice_fusion.2
  216.5 0.7 fusion.77
  219.0 0.7 maximum_dynamic-update-slice_fusion.2
  219.9 0.7 fusion.77
  223.3 0.7 fusion.77
  225.8 0.7 maximum_dynamic-update-slice_fusion.2
  226.7 0.7 fusion.77
  236.0 0.7 maximum_dynamic-update-slice_fusion.2
  239.4 0.7 maximum_dynamic-update-slice_fusion.2
  240.4 0.7 fusion.77
  242.8 0.7 maximum_dynamic-update-slice_fusion.2
  243.8 0.7 fusion.77
  246.2 0.7 maximum_dynamic-update-slice_fusion.2
  247.2 0.7 fusion.77
  249.7 0.7 maximum_dynamic-update-slice_fusion.2
  250.6 0.7 fusion.77
  253.1 0.7 maximum_dynamic-update-slice_fusion.2
  260.6 5.0 negate_convert_fusion
  265.6 11.1 %reshape.127 = bf16[16384,1,3]{2,1,0:T(2,128)(2,1)} reshape(bf16[16,2,1536]{2,1,0:T(2,128)(2,1)S(1)} %all-to-all-done) | data formatting | bytes 196608
  276.6 15.5 %copy.25 = bf16[1,3,16384]{2,1,0:T(4,128)(2,1)S(1)} copy(bf16[1,3,16384]{1,0,2:T(2,128)(2,1)} %bitcast.72) | data formatting | bytes 196608 | tf_op jit(solution)/shard_map/all_to_all | solution.py:88
  292.2 1.5 collective-permute-start
  293.7 1.8 sine_negate_fusion
  295.5 12.8 %copy.28 = bf16[16,32,3,1024]{1,0,2,3:T(8,128)(2,1)} copy(bf16[16,32,3,1024]{3,1,2,0:T(8,128)(2,1)S(1)} %copy-done.1) | data formatting | bytes 6291456 | tf_op jit(solution)/shard_map/while | solution.py:99
  308.6 1.8 convolution_convert_fusion
  310.3 0.8 fusion.61
  311.2 3.8 copy.38
  315.0 3.5 copy.37
  318.6 4.0 fusion.18
  322.6 6.7 %fusion.16 = f32[512,8,32,1]{2,1,3,0:T(8,128)} fusion(bf16[16,3,8,512]{0,2,1,3:T(8,128)(2,1)S(1)} %copy-done, bf16[16,32,3,1024]{1,0,2,3:T(8,128)(2,1)} %copy.28), kind=kOutput, calls=%fused_computation.23 | convolution fusion | flops 12582912 | bytes 7208960 | tf_op jit(solution)/shard_map/stcf,scnf->tnf/dot_general | solution.py:70
  329.4 3.1 fusion.25
  332.5 3.1 copy.31
  335.6 6.6 %fusion.24 = f32[32,8,512]{0,1,2:T(8,128)} fusion(f32[512,8,32,1]{2,1,3,0:T(8,128)} %fusion.16, bf16[16,3,8,512]{0,2,1,3:T(8,128)(2,1)S(1)} %copy.38, bf16[16,32,3,1024]{1,0,2,3:T(8,128)(2,1)} %copy.28), kind=kOutput, calls=%fused_computation.32 | convolution fusion | flops 12713984 | bytes 9306112 | tf_op jit(solution)/shard_map/stcf,scnf->tnf/dot_general | solution.py:68
  342.2 2.4 copy.32
  344.6 2.1 fusion.36
  347.4 1.3 dynamic-slice
  348.7 268.2 %all-reduce.3.cloned.1.call-done = f32[32,1024]{1,0:T(8,128)} async-done(((f32[32,1024]{1,0:T(8,128)}), f32[32,1024]{1,0:T(8,128)}) %all-reduce.3.cloned.1.call-update) | async-done | bytes 131088
  616.9 1.9 constant_dynamic-slice_fusion.1
  (107 shorter events, 30.1 us)
Async XLA Ops:
  113.1 27.9 %copy-start.3 = (bf16[1,32,3,256]{3,1,2,0:T(8,128)(2,1)S(1)}, bf16[1,32,3,256]{3,1,2,0:T(8,128)(2,1)}, u32[]{:S(2)}) copy-start(bf16[1,32,3,256]{3,1,2,0:T(8,128)(2,1)} %param.7) | copy-start | bytes 147460
  113.1 92.9 %copy-start.4 = (s32[16]{0:T(128)S(1)}, s32[16]{0:T(128)}, u32[]{:S(2)}) copy-start(s32[16]{0:T(128)} %param.9) | copy-start | bytes 196
  120.6 145.0 %all-to-all-start = ((bf16[16,2,1536]{2,1,0:T(2,128)(2,1)}), bf16[16,2,1536]{2,1,0:T(2,128)(2,1)S(1)}, u32[]{:S(2)}, u32[]{:S(2)}) async-start(bf16[16,2,1536]{2,1,0:T(2,128)(2,1)} %reshape.126), calls=%async_computation | async-start | bytes 196608 | tf_op jit(solution)/shard_map/all_to_all | solution.py:88
  138.8 478.1 %all-reduce.3.cloned.1.call-start = ((), (), s32[]{:S(2)}) async-start(), calls=%async_computation.1 | async-start | bytes 262144
  276.6 18.9 %copy-start.1 = (bf16[16,32,3,1024]{3,1,2,0:T(8,128)(2,1)S(1)}, bf16[16,32,3,1024]{3,1,2,0:T(8,128)(2,1)}, u32[]{:S(2)}) copy-start(bf16[16,32,3,1024]{3,1,2,0:T(8,128)(2,1)} %get-tuple-element.83) | copy-start | bytes 9437188
  292.2 16.0 %collective-permute-start = (bf16[16,3,384]{2,0,1:T(8,128)(2,1)S(1)}, bf16[16,3,384]{2,0,1:T(8,128)(2,1)S(1)}, u32[]{:S(2)}, u32[]{:S(2)}) collective-permute-start(bf16[16,3,384]{2,0,1:T(8,128)(2,1)S(1)} %slice.50), channel_id=1, source_target_pairs={{32,0},{64,32},{96,64},{128,96},{160,128},{192,160},{224,192},{256... | collective-permute-start | bytes 110600 | tf_op jit(solution)/shard_map/ppermute | solution.py:17
  318.6 4.0 copy-start
  318.6 10.8 %slice-start = ((s8[12582912]{0:T(1024)(128)(4,1)}), s8[4194304]{0:T(1024)(128)(4,1)S(1)}, s32[]{:S(2)}) async-start(s8[12582912]{0:T(1024)(128)(4,1)} %bitcast.69), calls=%async_computation.2 | async-start | bytes 8388608
  318.6 10.8 %slice-start.1 = ((s8[12582912]{0:T(1024)(128)(4,1)}), s8[4194304]{0:T(1024)(128)(4,1)S(1)}, s32[]{:S(2)}) async-start(s8[12582912]{0:T(1024)(128)(4,1)} %bitcast.69), calls=%async_computation.3 | async-start | bytes 8388608
  322.6 6.8 %slice-start.2 = ((s8[12582912]{0:T(1024)(128)(4,1)}), s8[4194304]{0:T(1024)(128)(4,1)S(1)}, s32[]{:S(2)}) async-start(s8[12582912]{0:T(1024)(128)(4,1)} %bitcast.69), calls=%async_computation.4 | async-start | bytes 8388608
  335.6 9.0 %copy-start.2 = (f32[512,128]{1,0:T(8,128)S(1)}, f32[512,128]{1,0:T(8,128)}, u32[]{:S(2)}) copy-start(f32[512,128]{1,0:T(8,128)} %get-tuple-element.110) | copy-start | bytes 786436
Sparse Core Ops, SparseCore 0:
  347.6 269.3 all-reduce.2
where the time goes:
time: 628 us; the launch traced here: 626 us
  waiting for transfers between devices  268 us (43%)
  other arithmetic  118 us (19%)
  local copies, waits for them, and re-layouts  102 us (16%)
  blocking collectives  64.9 us (10%)
  matrix products  27.8 us (4%)
  starting transfers between devices  19.7 us (3%)
  between operations  13.6 us (2%)
  loops' own time  11.3 us (2%)
    unnamed x2, waiting for transfers between devices  268 us
    unnamed x2, other arithmetic  90.8 us
    all_gather x1, blocking collectives, per_device(): lax.all_gather(templates, 'tm', axis=0, tiled=True)  64.9 us
    unnamed x25, local copies, waits for them, and re-layouts  45 us
    all_to_all x1, starting transfers between devices, per_device(): lax.all_to_all(seismic, 'tm', split_axis=2, concat_axis=0, tiled=True)  18.2 us
    all_to_all x1, local copies, waits for them, and re-layouts, per_device(): lax.all_to_all(seismic, 'tm', split_axis=2, concat_axis=0, tiled=True)  15.5 us
    while x1, local copies, waits for them, and re-layouts, per_device(): lax.map(one_station, (lax.all_gather(templates, 'tm', axis=0, tiled=True)...  12.8 us
  transfers between devices with their start and end apart: 3, of which 1 were waited for; matrix products, arithmetic and copies ran while one was open for 11% of the time, Pallas kernels for 0%

commit v1 on v0

v1 whole, which is shorter than its diff:
```python
import jax
import jax.numpy as jnp
from jax import lax
from jax.experimental import pallas as pl
from jax.experimental.pallas import tpu as pltpu
from jax.sharding import PartitionSpec as P

XS, ZH = 4, 4
YS, ZL, CORES = 4, 4, 2
CH = 3
L = 256
NF = 512
BLK = 128
TPL = 32
LANES = 128
SUB = 8
MESH = pl.DeviceIdType.MESH


def gather_kernel(seis_ref, wave_ref, xs_ref, tg_ref, send_sem, recv_sem, local_sem):
    tm = lax.axis_index("tm")
    x, zh = tm // ZH, tm % ZH
    quarter = (seis_ref.shape[1] - NF) // XS
    span = xs_ref.shape[2]

    def segment(px):
        return seis_ref.at[:, pl.ds(pl.multiple_of(px * quarter, LANES), span)]

    peers = [(x + d) % XS for d in range(1, XS)]
    barrier = pltpu.get_barrier_semaphore()
    for px in peers:
        pl.semaphore_signal(barrier, inc=1, device_id={"tm": px * ZH + zh}, device_id_type=MESH)
    pl.semaphore_wait(barrier, XS - 1)
    copies = []
    for d, px in enumerate(peers):
        target = {"tm": px * ZH + zh}
        copies.append(pltpu.make_async_remote_copy(
            src_ref=wave_ref, dst_ref=tg_ref.at[x], send_sem=send_sem.at[0, d],
            recv_sem=recv_sem.at[0, d], device_id=target, device_id_type=MESH))
        copies.append(pltpu.make_async_remote_copy(
            src_ref=segment(px), dst_ref=xs_ref.at[x], send_sem=send_sem.at[1, d],
            recv_sem=recv_sem.at[1, d], device_id=target, device_id_type=MESH))
    copies.append(pltpu.make_async_copy(wave_ref, tg_ref.at[x], local_sem.at[0]))
    copies.append(pltpu.make_async_copy(segment(x), xs_ref.at[x], local_sem.at[1]))
    for copy in copies:
        copy.start()
    for copy in copies:
        copy.wait()


def correlate_kernel(shift_ref, active_ref, tg_ref, xs_ref, out_ref, rows_ref, moved_ref, w_ref, f_ref):
    zh = lax.axis_index("tm") % ZH
    nrows = xs_ref.shape[2] // LANES
    out_ref[...] = jnp.zeros_like(out_ref)

    def station(s, carry):
        scale = active_ref[s * ZH + zh].astype(jnp.float32)
        signal = xs_ref[s].astype(jnp.float32) * scale
        for c in range(CH):
            for r in range(nrows):
                rows_ref[c, r : r + 1, :] = signal[c : c + 1, r * LANES : (r + 1) * LANES]
        for t in range(TPL):
            wave = tg_ref[s, t].astype(jnp.float32)
            wide = jnp.concatenate([wave, jnp.zeros((CH, NF - L), jnp.float32)], axis=1)
            moved_ref[t, 0:CH, :] = pltpu.roll(wide, shift_ref[s * ZH + zh, t], 1)
        for c in range(CH):
            frames = jnp.concatenate([rows_ref[c, u : u + 32, :] for u in range(NF // BLK)], axis=1)
            for j in range(0, 16, 2):
                even = frames if j == 0 else pltpu.roll(frames, NF - SUB * j, 1)
                odd = pltpu.roll(frames, NF - SUB * (j + 1), 1)
                for z in range(ZH):
                    top = z * LANES + SUB * j
                    both = jnp.concatenate(
                        [even[SUB * z : SUB * z + SUB], odd[SUB * z : SUB * z + SUB]], axis=0)
                    f_ref[top : top + 2 * SUB, :] = both.astype(jnp.bfloat16)
            for block in range(0, TPL, 2):
                pair = []
                for at in (block, block + 1):
                    t = (at % 16) * 2 + at // 16
                    wide = jnp.broadcast_to(moved_ref[t, c : c + 1, :], (SUB, NF))
                    pair.append(pltpu.roll(wide, 0, 1, stride=1, stride_axis=0))
                w_ref[block * SUB : (block + 2) * SUB, :] = jnp.concatenate(
                    pair, axis=0).astype(jnp.bfloat16)
            out_ref[...] += lax.dot_general(
                w_ref[...], f_ref[...], (((1,), (1,)), ((), ())),
                preferred_element_type=jnp.float32)
        return carry

    lax.fori_loop(0, XS, station, 0)


def reduce_kernel(part_ref, out_ref, half_ref, near_ref, sum_ref, plane_ref, far_ref,
                  s1, r1, s2, r2, s3, r3):
    tm, tmpl = lax.axis_index("tm"), lax.axis_index("tmpl")
    x, zh = tm // ZH, tm % ZH
    y, zl, core = tmpl // (ZL * CORES), (tmpl // CORES) % ZL, tmpl % CORES
    half = part_ref.shape[0] // CORES
    block = half // YS

    def place(py, pzl, pcore, pzh):
        return {"tm": x * ZH + pzh, "tmpl": py * (ZL * CORES) + pzl * CORES + pcore}

    other = place(y, zl, 1 - core, zh)
    ys = [((y + d) % YS, place((y + d) % YS, zl, core, zh)) for d in range(1, YS)]
    zs = []
    for d in range(1, ZL * ZH):
        pzl, pzh = (zl + d % ZL) % ZL, (zh + d // ZL) % ZH
        zs.append((pzl, pzh, place(y, pzl, core, pzh)))
    barrier = pltpu.get_barrier_semaphore()
    for target in [other] + [p[-1] for p in ys] + [p[-1] for p in zs]:
        pl.semaphore_signal(barrier, inc=1, device_id=target, device_id_type=MESH)
    pl.semaphore_wait(barrier, 1 + len(ys) + len(zs))

    first = pltpu.make_async_remote_copy(
        src_ref=part_ref.at[pl.ds(pl.multiple_of((1 - core) * half, SUB), half)], dst_ref=half_ref,
        send_sem=s1, recv_sem=r1, device_id=other, device_id_type=MESH)
    first.start()
    first.wait()
    sum_ref[...] = part_ref[pl.ds(pl.multiple_of(core * half, SUB), half)] + half_ref[...]

    second = [
        pltpu.make_async_remote_copy(
            src_ref=sum_ref.at[pl.ds(pl.multiple_of(py * block, SUB), block)],
            dst_ref=near_ref.at[d], send_sem=s2.at[d], recv_sem=r2.at[d],
            device_id=target, device_id_type=MESH)
        for d, (py, target) in enumerate(ys)]
    for copy in second:
        copy.start()
    for copy in second:
        copy.wait()
    plane_ref[...] = (sum_ref[pl.ds(pl.multiple_of(y * block, SUB), block)]
                      + near_ref[0] + near_ref[1] + near_ref[2])

    def tile(pzl, pzh):
        return (pl.ds(pl.multiple_of(pzl * SUB, SUB), SUB),
                pl.ds(pl.multiple_of(pzh * LANES, LANES), LANES))

    third = [
        pltpu.make_async_remote_copy(
            src_ref=plane_ref.at[tile(pzl, pzh)], dst_ref=far_ref.at[d],
            send_sem=s3.at[d], recv_sem=r3.at[d], device_id=target, device_id_type=MESH)
        for d, (pzl, pzh, target) in enumerate(zs)]
    for copy in third:
        copy.start()
    for copy in third:
        copy.wait()
    total = plane_ref[tile(zl, zh)]
    for d in range(len(zs)):
        total = total + far_ref[d]
    out_ref[...] = total


def vmem(count):
    return [pl.BlockSpec(memory_space=pltpu.VMEM)] * count


def per_device(seismic, templates, moveout, active):
    window = seismic.shape[2]
    span = window // XS + NF
    padded = jnp.pad(seismic[0], ((0, 0), (0, NF)))
    dma = pltpu.SemaphoreType.DMA
    xs, tg = pl.pallas_call(
        gather_kernel,
        out_shape=(jax.ShapeDtypeStruct((XS, CH, span), jnp.bfloat16),
                   jax.ShapeDtypeStruct((XS, TPL, CH, L), jnp.bfloat16)),
        in_specs=vmem(2), out_specs=tuple(vmem(2)),
        scratch_shapes=[dma((2, XS - 1)), dma((2, XS - 1)), dma((2,))],
        compiler_params=pltpu.CompilerParams(collective_id=0, has_side_effects=True),
        name="gather_x",
    )(padded, templates[0])

    rows, columns = TPL * SUB, window // XS // SUB
    part = pl.pallas_call(
        correlate_kernel,
        out_shape=jax.ShapeDtypeStruct((rows, columns), jnp.float32),
        in_specs=[pl.BlockSpec(memory_space=pltpu.SMEM)] * 2 + vmem(2),
        out_specs=vmem(1)[0],
        scratch_shapes=[pltpu.VMEM((CH, 40, LANES), jnp.float32),
                        pltpu.VMEM((TPL, SUB, NF), jnp.float32),
                        pltpu.VMEM((rows, NF), jnp.bfloat16),
                        pltpu.VMEM((columns, NF), jnp.bfloat16)],
        name="correlate",
    )(moveout, active, tg, xs)

    half = rows // CORES
    block = half // YS
    others = ZL * ZH - 1
    tile = pl.pallas_call(
        reduce_kernel,
        out_shape=jax.ShapeDtypeStruct((SUB, LANES), jnp.float32),
        in_specs=vmem(1), out_specs=vmem(1)[0],
        scratch_shapes=[pltpu.VMEM((half, columns), jnp.float32),
                        pltpu.VMEM((YS - 1, block, columns), jnp.float32),
                        pltpu.VMEM((half, columns), jnp.float32),
                        pltpu.VMEM((block, columns), jnp.float32),
                        pltpu.VMEM((others, SUB, LANES), jnp.float32),
                        dma, dma, dma((YS - 1,)), dma((YS - 1,)), dma((others,)), dma((others,))],
        compiler_params=pltpu.CompilerParams(collective_id=1, has_side_effects=True),
        name="reduce_scatter",
    )(part)
    return tile.reshape(SUB, LANES // SUB, SUB).transpose(2, 1, 0).reshape(1, SUB * LANES)


def solution(mesh):
    in_specs = (
        P(("tmpl", "tm"), None, None),
        P(("tmpl", "tm"), None, None, None),
        P("tmpl", None),
        P("tmpl"),
    )
    out_specs = P("tmpl", "tm")
    return jax.shard_map(
        per_device, mesh=mesh, in_specs=in_specs, out_specs=out_specs, check_vma=False
    )
```

time: 628 us -> 54.5 us (0.09)
  waiting for transfers between devices: 268 us -> 0 us
  other arithmetic: 118 us -> 0 us
  local copies, waits for them, and re-layouts: 102 us -> 4.62 us
  blocking collectives: 64.9 us -> 0 us
  Pallas kernels: 0 us -> 49.5 us
  matrix products: 27.8 us -> 0 us
  starting transfers between devices: 19.7 us -> 0 us
  between operations: 13.6 us -> 0.03 us
  loops' own time: 11.3 us -> 0 us
    unnamed x2 -> x0, waiting for transfers between devices: 268 us -> none
    unnamed x2 -> x0, other arithmetic: 90.8 us -> none
    all_gather x1 -> x0, blocking collectives: 64.9 us -> none  [per_device(): lax.all_gather(templates, 'tm', axis=0, tiled=True)]
    pallas_call x0 -> x3, Pallas kernels: none -> 49.5 us  [the longest x1 33.5 us: per_device(): pl.pallas_call(reduce_kernel, out_shape=jax.ShapeDtypeStruct((SUB, LANES)...]
    unnamed x25 -> x1, local copies, waits for them, and re-layouts: 45 us -> 1.46 us
    dot_general x22 -> x0, matrix products: 27.8 us -> none  [the longest x1 6.74 us: accumulate(): jnp.einsum('stcf,scnf->tnf', g_imag, x_real, preferred_element_type=jnp.f...]
    all_to_all x1 -> x0, starting transfers between devices: 18.2 us -> none  [per_device(): lax.all_to_all(seismic, 'tm', split_axis=2, concat_axis=0, tiled=True)]
    all_to_all x1 -> x0, local copies, waits for them, and re-layouts: 15.5 us -> none  [per_device(): lax.all_to_all(seismic, 'tm', split_axis=2, concat_axis=0, tiled=True)]
  transfers between devices with their start and end apart: 3 -> 0, of which waited for: 1 -> 0; matrix products, arithmetic and copies ran while one was open for 11% -> 0% of each run, Pallas kernels for 0% -> 0%
where the time goes in v1:
time: 54.5 us; the launch traced here: 54.1 us
  Pallas kernels  49.5 us (91%)
  local copies, waits for them, and re-layouts  4.62 us (8%)
    pallas_call x1, Pallas kernels, per_device(): pl.pallas_call(reduce_kernel, out_shape=jax.ShapeDtypeStruct((SUB, LANES)...  33.5 us
    pallas_call x1, Pallas kernels, per_device(): pl.pallas_call(gather_kernel, out_shape=(jax.ShapeDtypeStruct((XS, CH, sp...  10.1 us
    pallas_call x1, Pallas kernels, per_device(): pl.pallas_call(correlate_kernel, out_shape=jax.ShapeDtypeStruct((rows, co...  5.83 us
    pad x1, local copies, waits for them, and re-layouts, per_device(): padded = jnp.pad(seismic[0], ((0, 0), (0, NF)))  1.61 us
    unnamed x1, local copies, waits for them, and re-layouts  1.46 us
    reshape x2, local copies, waits for them, and re-layouts, per_device(): tile.reshape(SUB, LANES // SUB, SUB).transpose(2, 1, 0)  1.45 us

profile of v1, /device:TPU:1, one launch (start us, length us, event | category | flops | bytes accessed | tf_op | source)
XLA Modules:
  0.0 54.1 jit_solution(7789890312906807078)
XLA Ops:
  0.0 1.5 %copy.10 = bf16[1,32,3,256]{3,2,1,0:T(4,128)(2,1)} copy(bf16[1,32,3,256]{3,1,2,0:T(8,128)(2,1)} %param.5) | data formatting | bytes 98304 | tf_op args[1]
  1.5 1.6 %pad.4.seis_ref = bf16[3,16896]{1,0:T(4,128)(2,1)} pad(bf16[3,16384]{1,0:T(4,128)(2,1)} %bitcast.7, bf16[]{:T(256)} %constant.2.clone.1), padding=0_0x0_512 | pad | bytes 199682 | tf_op jit(solution)/shard_map/jit(_pad)/pad | solution.py:160
  3.1 10.1 %gather_x.1 = (bf16[4,3,4608]{2,1,0:T(4,128)(2,1)}, bf16[4,32,3,256]{3,2,1,0:T(4,128)(2,1)}) custom-call(bf16[3,16896]{1,0:T(4,128)(2,1)} %pad.4.seis_ref, bf16[32,3,256]{2,1,0:T(4,128)(2,1)} %bitcast.5), custom_call_target="tpu_custom_call" | custom-call | tf_op jit(solution)/shard_map/gather_x/pallas_call | solution.py:162
  13.2 5.8 %correlate.1.part_ref = f32[256,512]{1,0:T(8,128)} custom-call(s32[16,32]{1,0:T(8,128)} %shift_ref.1, s32[16]{0:T(128)} %active_ref.1, bf16[4,32,3,256]{3,2,1,0:T(4,128)(2,1)} %get-tuple-element.7.tg_ref, bf16[4,3,4608]{2,1,0:T(4,128)(2,1)} %get-tuple-element.8.xs_ref), custom_call_target="tpu_custom_call" | custom-call | tf_op jit(solution)/shard_map/correlate/pallas_call | solution.py:173
  19.0 33.5 %reduce_scatter.1 = f32[8,128]{1,0:T(8,128)} custom-call(f32[256,512]{1,0:T(8,128)} %correlate.1.part_ref), custom_call_target="tpu_custom_call" | custom-call | tf_op jit(solution)/shard_map/reduce_scatter/pallas_call | solution.py:188
  52.6 0.8 %reshape.6 = f32[8,16,8]{2,1,0:T(8,128)S(1)} reshape(f32[8,128]{1,0:T(8,128)} %reduce_scatter.1) | data formatting | bytes 8192 | tf_op jit(solution)/shard_map/reshape | solution.py:201
  53.3 0.1 copy.8
  53.4 0.7 %reshape.7 = f32[1,1024]{1,0:T(1,128)} reshape(f32[8,16,8]{2,1,0:T(8,128)S(1)} %copy.8) | data formatting | bytes 8192 | tf_op jit(solution)/shard_map/reshape | solution.py:201

commit v2 on v1

v2 whole, which is shorter than its diff:
```python
import jax
import jax.numpy as jnp
from jax import lax
from jax.experimental import pallas as pl
from jax.experimental.pallas import tpu as pltpu
from jax.sharding import PartitionSpec as P

XS, ZH = 4, 4
YS, ZL, CORES = 4, 4, 2
CH = 3
L = 256
NF = 512
BLK = 128
TPL = 32
LANES = 128
SUB = 8
MESH = pl.DeviceIdType.MESH


def gather_kernel(seis_ref, wave_ref, xs_ref, tg_ref, send_sem, recv_sem, local_sem):
    tm = lax.axis_index("tm")
    x, zh = tm // ZH, tm % ZH
    quarter = (seis_ref.shape[1] - NF) // XS
    span = xs_ref.shape[2]

    def segment(px):
        return seis_ref.at[:, pl.ds(pl.multiple_of(px * quarter, LANES), span)]

    peers = [(x + d) % XS for d in range(1, XS)]
    barrier = pltpu.get_barrier_semaphore()
    for px in peers:
        pl.semaphore_signal(barrier, inc=1, device_id={"tm": px * ZH + zh}, device_id_type=MESH)
    pl.semaphore_wait(barrier, XS - 1)
    copies = []
    for d, px in enumerate(peers):
        target = {"tm": px * ZH + zh}
        copies.append(pltpu.make_async_remote_copy(
            src_ref=wave_ref, dst_ref=tg_ref.at[x], send_sem=send_sem.at[0, d],
            recv_sem=recv_sem.at[0, d], device_id=target, device_id_type=MESH))
        copies.append(pltpu.make_async_remote_copy(
            src_ref=segment(px), dst_ref=xs_ref.at[x], send_sem=send_sem.at[1, d],
            recv_sem=recv_sem.at[1, d], device_id=target, device_id_type=MESH))
    copies.append(pltpu.make_async_copy(wave_ref, tg_ref.at[x], local_sem.at[0]))
    copies.append(pltpu.make_async_copy(segment(x), xs_ref.at[x], local_sem.at[1]))
    for copy in copies:
        copy.start()
    for copy in copies:
        copy.wait()


def transpose_groups(tile):
    row = lax.broadcasted_iota(jnp.int32, tile.shape, 0)
    lane = lax.broadcasted_iota(jnp.int32, tile.shape, 1)
    for bit in (1, 2, 4):
        below = pltpu.roll(pltpu.roll(tile, SUB - bit, 0), bit, 1)
        above = pltpu.roll(pltpu.roll(tile, bit, 0), LANES - bit, 1)
        low, left = (row & bit) == 0, (lane & bit) == 0
        tile = jnp.where(low == left, tile, jnp.where(low, below, above))
    return tile


def correlate_kernel(shift_ref, active_ref, tg_ref, xs_ref, out_ref,
                     rows_ref, moved_ref, w_ref, f_ref, acc_ref,
                     core_send, core_recv, sum_ref, y_send, y_recv, plane_ref, z_send, z_recv,
                     s1, r1, s2, r2, s3, r3):
    tm, tmpl = lax.axis_index("tm"), lax.axis_index("tmpl")
    x, zh = tm // ZH, tm % ZH
    y, zl, core = tmpl // (ZL * CORES), (tmpl // CORES) % ZL, tmpl % CORES
    nz = ZL * ZH
    z = zh * ZL + zl
    half = acc_ref.shape[1] // CORES
    block = half // YS

    def place(py, pz, pcore):
        return {"tm": x * ZH + pz // ZL, "tmpl": py * (ZL * CORES) + (pz % ZL) * CORES + pcore}

    other = place(y, z, 1 - core)
    ys = [(d - 1, (y + d) % YS) for d in (2, 1, 3)]
    zs = [(d - 1, (z + d) % nz) for d in sorted(range(1, nz), key=lambda d: abs(d - nz // 2))]
    barrier = pltpu.get_barrier_semaphore()
    targets = [place(y, pz, core) for _, pz in zs] + [place(py, z, core) for _, py in ys] + [other]
    for target in targets:
        pl.semaphore_signal(barrier, inc=1, device_id=target, device_id_type=MESH)

    acc_ref[...] = jnp.zeros_like(acc_ref)
    nrows = xs_ref.shape[2] // LANES

    def multiply(s, c, part):
        frames = jnp.concatenate(
            [rows_ref[s, c, u + 16 * part : u + 16 * part + 16, :] for u in range(NF // BLK)], axis=1)
        for j in range(0, 16, 2):
            even = frames if j == 0 else pltpu.roll(frames, NF - SUB * j, 1)
            odd = pltpu.roll(frames, NF - SUB * (j + 1), 1)
            for k in range(2):
                top = k * LANES + SUB * j
                both = jnp.concatenate(
                    [even[SUB * k : SUB * k + SUB], odd[SUB * k : SUB * k + SUB]], axis=0)
                f_ref[top : top + 2 * SUB, :] = both.astype(jnp.bfloat16)
        acc_ref[part] += lax.dot_general(
            w_ref[s, c], f_ref[...], (((1,), (1,)), ((), ())), preferred_element_type=jnp.float32)

    def early(s, carry):
        scale = active_ref[s * ZH + zh].astype(jnp.float32)
        signal = xs_ref[s].astype(jnp.float32) * scale
        for c in range(CH):
            for r in range(nrows):
                rows_ref[s, c, r : r + 1, :] = signal[c : c + 1, r * LANES : (r + 1) * LANES]
        for t in range(TPL):
            wave = tg_ref[s, t].astype(jnp.float32)
            wide = jnp.concatenate([wave, jnp.zeros((CH, NF - L), jnp.float32)], axis=1)
            moved_ref[t, 0:CH, :] = pltpu.roll(wide, shift_ref[s * ZH + zh, t], 1)
        for c in range(CH):
            for at in range(0, TPL, 2):
                pair = []
                for slot in (at, at + 1):
                    t = (slot % 16) * 2 + slot // 16
                    wide = jnp.broadcast_to(moved_ref[t, c : c + 1, :], (SUB, NF))
                    pair.append(pltpu.roll(wide, 0, 1, stride=1, stride_axis=0))
                w_ref[s, c, at * SUB : (at + 2) * SUB, :] = jnp.concatenate(
                    pair, axis=0).astype(jnp.bfloat16)
            multiply(s, c, 0)
        return carry

    def late(s, carry):
        for c in range(CH):
            multiply(s, c, 1)
        return carry

    away = pl.ds(pl.multiple_of((1 - core) * half, SUB), half)
    mine = pl.ds(pl.multiple_of(core * half, SUB), half)

    def to_core(part):
        return pltpu.make_async_remote_copy(
            src_ref=core_send.at[part], dst_ref=core_recv.at[part], send_sem=s1.at[part],
            recv_sem=r1.at[part], device_id=other, device_id_type=MESH)

    lax.fori_loop(0, XS, early, 0)
    core_send[0] = acc_ref[0, away].astype(jnp.bfloat16)
    pl.semaphore_wait(barrier, len(targets))
    to_core(0).start()
    lax.fori_loop(0, XS, late, 0)
    core_send[1] = acc_ref[1, away].astype(jnp.bfloat16)
    to_core(1).start()

    def to_y(part, d, py):
        return pltpu.make_async_remote_copy(
            src_ref=y_send.at[part, pl.ds(pl.multiple_of(py * block, block), block)],
            dst_ref=y_recv.at[part, d], send_sem=s2.at[part, d], recv_sem=r2.at[part, d],
            device_id=place(py, z, core), device_id_type=MESH)

    for part in range(2):
        to_core(part).wait()
        total = acc_ref[part, mine] + core_recv[part].astype(jnp.float32)
        sum_ref[part] = total
        y_send[part] = total.astype(jnp.bfloat16)
        for d, py in ys:
            to_y(part, d, py).start()

    for part in range(2):
        total = sum_ref[part, pl.ds(pl.multiple_of(y * block, block), block)]
        for d, py in ys:
            to_y(part, d, py).wait()
            total = total + y_recv[part, d].astype(jnp.float32)
        for pzl in range(ZL):
            for k in range(2):
                tile = total[pzl * SUB : (pzl + 1) * SUB, k * LANES : (k + 1) * LANES]
                at = (2 * part + k) * ZL + pzl
                plane_ref[at] = tile
                z_send[at] = tile.astype(jnp.bfloat16)

    last = [
        pltpu.make_async_remote_copy(
            src_ref=z_send.at[pz], dst_ref=z_recv.at[d], send_sem=s3.at[d], recv_sem=r3.at[d],
            device_id=place(y, pz, core), device_id_type=MESH)
        for d, pz in zs]
    for copy in last:
        copy.start()
    for copy in last:
        copy.wait()
    total = plane_ref[z]
    for d in range(nz - 1):
        total = total + z_recv[d].astype(jnp.float32)
    out_ref[...] = transpose_groups(total)


def vmem(count):
    return [pl.BlockSpec(memory_space=pltpu.VMEM)] * count


def per_device(seismic, templates, moveout, active):
    window = seismic.shape[2]
    span = window // XS + NF
    padded = jnp.pad(seismic[0], ((0, 0), (0, NF)))
    dma = pltpu.SemaphoreType.DMA
    xs, tg = pl.pallas_call(
        gather_kernel,
        out_shape=(jax.ShapeDtypeStruct((XS, CH, span), jnp.bfloat16),
                   jax.ShapeDtypeStruct((XS, TPL, CH, L), jnp.bfloat16)),
        in_specs=vmem(2), out_specs=tuple(vmem(2)),
        scratch_shapes=[dma((2, XS - 1)), dma((2, XS - 1)), dma((2,))],
        compiler_params=pltpu.CompilerParams(collective_id=0, has_side_effects=True),
        name="gather_x",
    )(padded, templates[0])

    rows, columns = TPL * SUB, window // XS // SUB // 2
    half = rows // CORES
    block = half // YS
    devices = ZL * ZH
    bf16, f32 = jnp.bfloat16, jnp.float32
    tile = pl.pallas_call(
        correlate_kernel,
        out_shape=jax.ShapeDtypeStruct((SUB, LANES), f32),
        in_specs=[pl.BlockSpec(memory_space=pltpu.SMEM)] * 2 + vmem(2),
        out_specs=vmem(1)[0],
        scratch_shapes=[pltpu.VMEM((XS, CH, 40, LANES), f32),
                        pltpu.VMEM((TPL, SUB, NF), f32),
                        pltpu.VMEM((XS, CH, rows, NF), bf16),
                        pltpu.VMEM((columns, NF), bf16),
                        pltpu.VMEM((2, rows, columns), f32),
                        pltpu.VMEM((2, half, columns), bf16),
                        pltpu.VMEM((2, half, columns), bf16),
                        pltpu.VMEM((2, half, columns), f32),
                        pltpu.VMEM((2, half, columns), bf16),
                        pltpu.VMEM((2, YS - 1, block, columns), bf16),
                        pltpu.VMEM((devices, SUB, LANES), f32),
                        pltpu.VMEM((devices, SUB, LANES), bf16),
                        pltpu.VMEM((devices - 1, SUB, LANES), bf16),
                        dma((2,)), dma((2,)), dma((2, YS - 1)), dma((2, YS - 1)),
                        dma((devices - 1,)), dma((devices - 1,))],
        compiler_params=pltpu.CompilerParams(collective_id=1, has_side_effects=True),
        name="correlate_reduce",
    )(moveout, active, tg, xs)
    return tile.reshape(1, SUB * LANES)


def solution(mesh):
    in_specs = (
        P(("tmpl", "tm"), None, None),
        P(("tmpl", "tm"), None, None, None),
        P("tmpl", None),
        P("tmpl"),
    )
    out_specs = P("tmpl", "tm")
    return jax.shard_map(
        per_device, mesh=mesh, in_specs=in_specs, out_specs=out_specs, check_vma=False
    )
```

time: 54.5 us -> 46.3 us (0.85)
  Pallas kernels: 49.5 us -> 41.7 us
    pallas_call x2 -> x1, Pallas kernels: 39.4 us -> 31.6 us  [per_device(): pl.pallas_call(correlate_kernel, out_shape=jax.ShapeDtypeStruct((SUB, LAN...]
    reshape x2 -> x0, local copies, waits for them, and re-layouts: 1.45 us -> none  [per_device(): tile.reshape(SUB, LANES // SUB, SUB).transpose(2, 1, 0)]
    unnamed x1 -> x2, local copies, waits for them, and re-layouts: 1.46 us -> 2.74 us
where the time goes in v2:
time: 46.3 us; the launch traced here: 46 us
  Pallas kernels  41.7 us (90%)
  local copies, waits for them, and re-layouts  4.34 us (9%)
    pallas_call x1, Pallas kernels, per_device(): pl.pallas_call(correlate_kernel, out_shape=jax.ShapeDtypeStruct((SUB, LAN...  31.6 us
    pallas_call x1, Pallas kernels, per_device(): pl.pallas_call(gather_kernel, out_shape=(jax.ShapeDtypeStruct((XS, CH, sp...  10.1 us
    unnamed x2, local copies, waits for them, and re-layouts  2.74 us
    pad x1, local copies, waits for them, and re-layouts, per_device(): padded = jnp.pad(seismic[0], ((0, 0), (0, NF)))  1.6 us

profile of v2, /device:TPU:1, one launch (start us, length us, event | category | flops | bytes accessed | tf_op | source)
XLA Modules:
  0.0 46.0 jit_solution(10978100736564953312)
XLA Ops:
  0.0 1.5 %copy.7 = bf16[1,32,3,256]{3,2,1,0:T(4,128)(2,1)} copy(bf16[1,32,3,256]{3,1,2,0:T(8,128)(2,1)} %param.5) | data formatting | bytes 98304 | tf_op args[1]
  1.5 1.6 %pad.4.seis_ref = bf16[3,16896]{1,0:T(4,128)(2,1)} pad(bf16[3,16384]{1,0:T(4,128)(2,1)} %bitcast.6, bf16[]{:T(256)} %constant.2.clone.1), padding=0_0x0_512 | pad | bytes 199682 | tf_op jit(solution)/shard_map/jit(_pad)/pad | solution.py:193
  3.1 10.1 %gather_x.1 = (bf16[4,3,4608]{2,1,0:T(4,128)(2,1)}, bf16[4,32,3,256]{3,2,1,0:T(4,128)(2,1)}) custom-call(bf16[3,16896]{1,0:T(4,128)(2,1)} %pad.4.seis_ref, bf16[32,3,256]{2,1,0:T(4,128)(2,1)} %bitcast.5), custom_call_target="tpu_custom_call" | custom-call | tf_op jit(solution)/shard_map/gather_x/pallas_call | solution.py:195
  13.2 31.6 %correlate_reduce.1 = f32[8,128]{1,0:T(8,128)} custom-call(s32[16,32]{1,0:T(8,128)} %shift_ref.1, s32[16]{0:T(128)} %active_ref.1, bf16[4,32,3,256]{3,2,1,0:T(4,128)(2,1)} %get-tuple-element.7.tg_ref, bf16[4,3,4608]{2,1,0:T(4,128)(2,1)} %get-tuple-element.8.xs_ref), custom_call_target="tpu_custom_call" | custom-call | tf_op jit(solution)/shard_map/correlate_reduce/pallas_call | solution.py:210
  44.7 1.3 %copy.9 = f32[1,1024]{1,0:T(1,128)} copy(f32[1,1024]{1,0:T(1,128)} %bitcast.7) | data formatting | bytes 8192

commit v3 on v2

--- a/solution.py
+++ b/solution.py
@@ -17,37 +17,6 @@
 MESH = pl.DeviceIdType.MESH
 
 
-def gather_kernel(seis_ref, wave_ref, xs_ref, tg_ref, send_sem, recv_sem, local_sem):
-    tm = lax.axis_index("tm")
-    x, zh = tm // ZH, tm % ZH
-    quarter = (seis_ref.shape[1] - NF) // XS
-    span = xs_ref.shape[2]
-
-    def segment(px):
-        return seis_ref.at[:, pl.ds(pl.multiple_of(px * quarter, LANES), span)]
-
-    peers = [(x + d) % XS for d in range(1, XS)]
-    barrier = pltpu.get_barrier_semaphore()
-    for px in peers:
-        pl.semaphore_signal(barrier, inc=1, device_id={"tm": px * ZH + zh}, device_id_type=MESH)
-    pl.semaphore_wait(barrier, XS - 1)
-    copies = []
-    for d, px in enumerate(peers):
-        target = {"tm": px * ZH + zh}
-        copies.append(pltpu.make_async_remote_copy(
-            src_ref=wave_ref, dst_ref=tg_ref.at[x], send_sem=send_sem.at[0, d],
-            recv_sem=recv_sem.at[0, d], device_id=target, device_id_type=MESH))
-        copies.append(pltpu.make_async_remote_copy(
-            src_ref=segment(px), dst_ref=xs_ref.at[x], send_sem=send_sem.at[1, d],
-            recv_sem=recv_sem.at[1, d], device_id=target, device_id_type=MESH))
-    copies.append(pltpu.make_async_copy(wave_ref, tg_ref.at[x], local_sem.at[0]))
-    copies.append(pltpu.make_async_copy(segment(x), xs_ref.at[x], local_sem.at[1]))
-    for copy in copies:
-        copy.start()
-    for copy in copies:
-        copy.wait()
-
-
 def transpose_groups(tile):
     row = lax.broadcasted_iota(jnp.int32, tile.shape, 0)
     lane = lax.broadcasted_iota(jnp.int32, tile.shape, 1)
@@ -59,10 +28,10 @@
     return tile
 
 
-def correlate_kernel(shift_ref, active_ref, tg_ref, xs_ref, out_ref,
-                     rows_ref, moved_ref, w_ref, f_ref, acc_ref,
-                     core_send, core_recv, sum_ref, y_send, y_recv, plane_ref, z_send, z_recv,
-                     s1, r1, s2, r2, s3, r3):
+def stack_kernel(shift_ref, active_ref, seis_ref, wave_ref, out_ref,
+                 xs_ref, tg_ref, gs, gr, gl, rows_ref, moved_ref, w_ref, f_ref, acc_ref,
+                 core_send, core_recv, sum_ref, y_send, y_recv, plane_ref, z_send, z_recv,
+                 s1, r1, s2, r2, s3, r3):
     tm, tmpl = lax.axis_index("tm"), lax.axis_index("tmpl")
     x, zh = tm // ZH, tm % ZH
     y, zl, core = tmpl // (ZL * CORES), (tmpl // CORES) % ZL, tmpl % CORES
@@ -71,6 +40,25 @@
     half = acc_ref.shape[1] // CORES
     block = half // YS
 
+    quarter = seis_ref.shape[1] // XS
+    halo = xs_ref.shape[2] - quarter
+
+    def along_x(px):
+        return {"tm": px * ZH + zh}
+
+    def pieces(px):
+        follow = (px + 1) % XS * quarter
+        return [
+            (seis_ref.at[:, pl.ds(pl.multiple_of(px * quarter, LANES), quarter)],
+             xs_ref.at[x, :, 0:quarter]),
+            (seis_ref.at[:, pl.ds(pl.multiple_of(follow, LANES), halo)],
+             xs_ref.at[x, :, quarter : quarter + halo])]
+
+    def send(kind, source, target, d, back):
+        return pltpu.make_async_remote_copy(
+            src_ref=source, dst_ref=target, send_sem=gs.at[kind, d], recv_sem=gr.at[kind, back],
+            device_id=along_x((x + d) % XS), device_id_type=MESH)
+
     def place(py, pz, pcore):
         return {"tm": x * ZH + pz // ZL, "tmpl": py * (ZL * CORES) + (pz % ZL) * CORES + pcore}
 
@@ -79,10 +67,17 @@
     zs = [(d - 1, (z + d) % nz) for d in sorted(range(1, nz), key=lambda d: abs(d - nz // 2))]
     barrier = pltpu.get_barrier_semaphore()
     targets = [place(y, pz, core) for _, pz in zs] + [place(py, z, core) for _, py in ys] + [other]
+    targets += [along_x((x + d) % XS) for d in range(1, XS)]
     for target in targets:
         pl.semaphore_signal(barrier, inc=1, device_id=target, device_id_type=MESH)
 
+    local = [pltpu.make_async_copy(wave_ref, tg_ref.at[x], gl.at[0])]
+    local += [pltpu.make_async_copy(*pair, gl.at[1 + k]) for k, pair in enumerate(pieces(x))]
+    for copy in local:
+        copy.start()
     acc_ref[...] = jnp.zeros_like(acc_ref)
+    for copy in local:
+        copy.wait()
     nrows = xs_ref.shape[2] // LANES
 
     def multiply(s, c, part):
@@ -99,14 +94,18 @@
         acc_ref[part] += lax.dot_general(
             w_ref[s, c], f_ref[...], (((1,), (1,)), ((), ())), preferred_element_type=jnp.float32)
 
-    def early(s, carry):
+    def early(s):
         scale = active_ref[s * ZH + zh].astype(jnp.float32)
-        signal = xs_ref[s].astype(jnp.float32) * scale
+        column = lax.broadcasted_iota(jnp.int32, xs_ref.shape[1:], 1)
+        last_quarter = jnp.full(xs_ref.shape[1:], x, jnp.int32) == XS - 1
+        past = jnp.logical_and(last_quarter, column >= quarter)
+        signal = jnp.where(past, 0.0, xs_ref[s].astype(jnp.float32) * scale)
         for c in range(CH):
             for r in range(nrows):
                 rows_ref[s, c, r : r + 1, :] = signal[c : c + 1, r * LANES : (r + 1) * LANES]
+        waves = [tg_ref[s, c].astype(jnp.float32) for c in range(CH)]
         for t in range(TPL):
-            wave = tg_ref[s, t].astype(jnp.float32)
+            wave = jnp.concatenate([w[t : t + 1] for w in waves], axis=0)
             wide = jnp.concatenate([wave, jnp.zeros((CH, NF - L), jnp.float32)], axis=1)
             moved_ref[t, 0:CH, :] = pltpu.roll(wide, shift_ref[s * ZH + zh, t], 1)
         for c in range(CH):
@@ -119,7 +118,6 @@
                 w_ref[s, c, at * SUB : (at + 2) * SUB, :] = jnp.concatenate(
                     pair, axis=0).astype(jnp.bfloat16)
             multiply(s, c, 0)
-        return carry
 
     def late(s, carry):
         for c in range(CH):
@@ -133,14 +131,6 @@
         return pltpu.make_async_remote_copy(
             src_ref=core_send.at[part], dst_ref=core_recv.at[part], send_sem=s1.at[part],
             recv_sem=r1.at[part], device_id=other, device_id_type=MESH)
-
-    lax.fori_loop(0, XS, early, 0)
-    core_send[0] = acc_ref[0, away].astype(jnp.bfloat16)
-    pl.semaphore_wait(barrier, len(targets))
-    to_core(0).start()
-    lax.fori_loop(0, XS, late, 0)
-    core_send[1] = acc_ref[1, away].astype(jnp.bfloat16)
-    to_core(1).start()
 
     def to_y(part, d, py):
         return pltpu.make_async_remote_copy(
@@ -148,13 +138,58 @@
             dst_ref=y_recv.at[part, d], send_sem=s2.at[part, d], recv_sem=r2.at[part, d],
             device_id=place(py, z, core), device_id_type=MESH)
 
-    for part in range(2):
+    def after_core(part):
         to_core(part).wait()
         total = acc_ref[part, mine] + core_recv[part].astype(jnp.float32)
         sum_ref[part] = total
         y_send[part] = total.astype(jnp.bfloat16)
         for d, py in ys:
             to_y(part, d, py).start()
+
+    gather = []
+    for d in (1, 3):
+        gather.append(send(0, wave_ref, tg_ref.at[x], d, XS - d))
+    for d in (1, 3, 2):
+        for k, (source, target) in enumerate(pieces((x + d) % XS)):
+            gather.append(send(1 + k, source, target, d, XS - d))
+    onward = tg_ref.at[(x + 1) % XS]
+    relay = pltpu.make_async_remote_copy(
+        src_ref=onward, dst_ref=onward, send_sem=gs.at[0, 2], recv_sem=gr.at[0, 2],
+        device_id=along_x((x + 3) % XS), device_id_type=MESH)
+    pl.semaphore_wait(barrier, len(targets))
+    for copy in gather:
+        copy.start()
+
+    def arrive(step, carry):
+        offset = step ^ (step // 2)
+        s = (x + offset) % XS
+
+        @pl.when(step > 0)
+        def _():
+            send(0, wave_ref, tg_ref.at[s], 1, offset).wait_recv()
+
+            @pl.when(step == 1)
+            def _():
+                relay.start()
+
+            for k, (source, _) in enumerate(pieces(x)):
+                target = xs_ref.at[s, :, k * quarter : k * quarter + source.shape[1]]
+                send(1 + k, source, target, 1, offset).wait_recv()
+
+        early(s)
+        return carry
+
+    lax.fori_loop(0, XS, arrive, 0)
+    for copy in gather + [relay]:
+        copy.wait_send()
+    core_send[0] = acc_ref[0, away].astype(jnp.bfloat16)
+    to_core(0).start()
+    lax.fori_loop(0, 2, late, 0)
+    after_core(0)
+    lax.fori_loop(2, XS, late, 0)
+    core_send[1] = acc_ref[1, away].astype(jnp.bfloat16)
+    to_core(1).start()
+    after_core(1)
 
     for part in range(2):
         total = sum_ref[part, pl.ds(pl.multiple_of(y * block, block), block)]
@@ -190,29 +225,21 @@
 def per_device(seismic, templates, moveout, active):
     window = seismic.shape[2]
     span = window // XS + NF
-    padded = jnp.pad(seismic[0], ((0, 0), (0, NF)))
     dma = pltpu.SemaphoreType.DMA
-    xs, tg = pl.pallas_call(
-        gather_kernel,
-        out_shape=(jax.ShapeDtypeStruct((XS, CH, span), jnp.bfloat16),
-                   jax.ShapeDtypeStruct((XS, TPL, CH, L), jnp.bfloat16)),
-        in_specs=vmem(2), out_specs=tuple(vmem(2)),
-        scratch_shapes=[dma((2, XS - 1)), dma((2, XS - 1)), dma((2,))],
-        compiler_params=pltpu.CompilerParams(collective_id=0, has_side_effects=True),
-        name="gather_x",
-    )(padded, templates[0])
-
     rows, columns = TPL * SUB, window // XS // SUB // 2
     half = rows // CORES
     block = half // YS
     devices = ZL * ZH
     bf16, f32 = jnp.bfloat16, jnp.float32
     tile = pl.pallas_call(
-        correlate_kernel,
+        stack_kernel,
         out_shape=jax.ShapeDtypeStruct((SUB, LANES), f32),
         in_specs=[pl.BlockSpec(memory_space=pltpu.SMEM)] * 2 + vmem(2),
         out_specs=vmem(1)[0],
-        scratch_shapes=[pltpu.VMEM((XS, CH, 40, LANES), f32),
+        scratch_shapes=[pltpu.VMEM((XS, CH, span), bf16),
+                        pltpu.VMEM((XS, CH, TPL, L), bf16),
+                        dma((3, XS)), dma((3, XS)), dma((3,)),
+                        pltpu.VMEM((XS, CH, 40, LANES), f32),
                         pltpu.VMEM((TPL, SUB, NF), f32),
                         pltpu.VMEM((XS, CH, rows, NF), bf16),
                         pltpu.VMEM((columns, NF), bf16),
@@ -227,9 +254,9 @@
                         pltpu.VMEM((devices - 1, SUB, LANES), bf16),
                         dma((2,)), dma((2,)), dma((2, YS - 1)), dma((2, YS - 1)),
                         dma((devices - 1,)), dma((devices - 1,))],
-        compiler_params=pltpu.CompilerParams(collective_id=1, has_side_effects=True),
-        name="correlate_reduce",
-    )(moveout, active, tg, xs)
+        compiler_params=pltpu.CompilerParams(collective_id=0, has_side_effects=True),
+        name="stack",
+    )(moveout, active, seismic[0], templates[0].transpose(1, 0, 2))
     return tile.reshape(1, SUB * LANES)
 
 

time: 46.3 us -> 40.1 us (0.87)
  Pallas kernels: 41.7 us -> 38.6 us
  local copies, waits for them, and re-layouts: 4.34 us -> 1.28 us
    pallas_call x2 -> x1, Pallas kernels: 41.7 us -> 38.6 us  [per_device(): pl.pallas_call(stack_kernel, out_shape=jax.ShapeDtypeStruct((SUB, LANES),...]
    pad x1 -> x0, local copies, waits for them, and re-layouts: 1.6 us -> none  [per_device(): padded = jnp.pad(seismic[0], ((0, 0), (0, NF)))]
    unnamed x2 -> x1, local copies, waits for them, and re-layouts: 2.74 us -> 1.28 us
where the time goes in v3:
time: 40.1 us; the launch traced here: 39.9 us
  Pallas kernels  38.6 us (96%)
  local copies, waits for them, and re-layouts  1.28 us (3%)
    pallas_call x1, Pallas kernels, per_device(): pl.pallas_call(stack_kernel, out_shape=jax.ShapeDtypeStruct((SUB, LANES),...  38.6 us
    unnamed x1, local copies, waits for them, and re-layouts  1.28 us

profile of v3, /device:TPU:1, one launch (start us, length us, event | category | flops | bytes accessed | tf_op | source)
XLA Modules:
  0.0 39.9 jit_solution(16841408468764755459)
XLA Ops:
  0.0 38.6 %stack.1 = f32[8,128]{1,0:T(8,128)} custom-call(s32[16,32]{1,0:T(8,128)} %shift_ref.1, s32[16]{0:T(128)} %active_ref.1, bf16[3,16384]{1,0:T(4,128)(2,1)} %bitcast.5, bf16[3,32,256]{2,1,0:T(8,128)(2,1)} %bitcast.6), custom_call_target="tpu_custom_call" | custom-call | tf_op jit(solution)/shard_map/stack/pallas_call | solution.py:234
  38.6 1.3 %copy.6 = f32[1,1024]{1,0:T(1,128)} copy(f32[1,1024]{1,0:T(1,128)} %bitcast.7) | data formatting | bytes 8192

commit v4 on v3

--- a/solution.py
+++ b/solution.py
@@ -31,7 +31,7 @@
 def stack_kernel(shift_ref, active_ref, seis_ref, wave_ref, out_ref,
                  xs_ref, tg_ref, gs, gr, gl, rows_ref, moved_ref, w_ref, f_ref, acc_ref,
                  core_send, core_recv, sum_ref, y_send, y_recv, plane_ref, z_send, z_recv,
-                 s1, r1, s2, r2, s3, r3):
+                 s1, r1, s2, r2, s3, r3, ready):
     tm, tmpl = lax.axis_index("tm"), lax.axis_index("tmpl")
     x, zh = tm // ZH, tm % ZH
     y, zl, core = tmpl // (ZL * CORES), (tmpl // CORES) % ZL, tmpl % CORES
@@ -59,6 +59,14 @@
             src_ref=source, dst_ref=target, send_sem=gs.at[kind, d], recv_sem=gr.at[kind, back],
             device_id=along_x((x + d) % XS), device_id_type=MESH)
 
+    def tell(reach):
+        for d in (reach, nz - reach):
+            pl.semaphore_signal(ready.at[reach // 2], inc=1, device_id=place(y, (z + d) % nz, core),
+                                device_id_type=MESH)
+
+    def heard(reach):
+        pl.semaphore_wait(ready.at[reach // 2], 2)
+
     def place(py, pz, pcore):
         return {"tm": x * ZH + pz // ZL, "tmpl": py * (ZL * CORES) + (pz % ZL) * CORES + pcore}
 
@@ -66,7 +74,8 @@
     ys = [(d - 1, (y + d) % YS) for d in (2, 1, 3)]
     zs = [(d - 1, (z + d) % nz) for d in sorted(range(1, nz), key=lambda d: abs(d - nz // 2))]
     barrier = pltpu.get_barrier_semaphore()
-    targets = [place(y, pz, core) for _, pz in zs] + [place(py, z, core) for _, py in ys] + [other]
+    targets = [place(y, (z + d) % nz, core) for d in (1, nz - 1)]
+    targets += [place(py, z, core) for _, py in ys] + [other]
     targets += [along_x((x + d) % XS) for d in range(1, XS)]
     for target in targets:
         pl.semaphore_signal(barrier, inc=1, device_id=target, device_id_type=MESH)
@@ -119,10 +128,9 @@
                     pair, axis=0).astype(jnp.bfloat16)
             multiply(s, c, 0)
 
-    def late(s, carry):
+    def late(s):
         for c in range(CH):
             multiply(s, c, 1)
-        return carry
 
     away = pl.ds(pl.multiple_of((1 - core) * half, SUB), half)
     mine = pl.ds(pl.multiple_of(core * half, SUB), half)
@@ -159,6 +167,7 @@
     pl.semaphore_wait(barrier, len(targets))
     for copy in gather:
         copy.start()
+    tell(1)
 
     def arrive(step, carry):
         offset = step ^ (step // 2)
@@ -176,20 +185,34 @@
                 target = xs_ref.at[s, :, k * quarter : k * quarter + source.shape[1]]
                 send(1 + k, source, target, 1, offset).wait_recv()
 
+        @pl.when(step == 1)
+        def _():
+            heard(1)
+            tell(2)
+
+        @pl.when(step == 2)
+        def _():
+            heard(2)
+            tell(4)
+
         early(s)
+
+        @pl.when(step < XS - 1)
+        def _():
+            late(s)
+
         return carry
 
     lax.fori_loop(0, XS, arrive, 0)
+    core_send[0] = acc_ref[0, away].astype(jnp.bfloat16)
+    to_core(0).start()
+    late((x + 2) % XS)
+    core_send[1] = acc_ref[1, away].astype(jnp.bfloat16)
+    to_core(1).start()
+    after_core(0)
+    after_core(1)
     for copy in gather + [relay]:
         copy.wait_send()
-    core_send[0] = acc_ref[0, away].astype(jnp.bfloat16)
-    to_core(0).start()
-    lax.fori_loop(0, 2, late, 0)
-    after_core(0)
-    lax.fori_loop(2, XS, late, 0)
-    core_send[1] = acc_ref[1, away].astype(jnp.bfloat16)
-    to_core(1).start()
-    after_core(1)
 
     for part in range(2):
         total = sum_ref[part, pl.ds(pl.multiple_of(y * block, block), block)]
@@ -208,6 +231,7 @@
             src_ref=z_send.at[pz], dst_ref=z_recv.at[d], send_sem=s3.at[d], recv_sem=r3.at[d],
             device_id=place(y, pz, core), device_id_type=MESH)
         for d, pz in zs]
+    heard(4)
     for copy in last:
         copy.start()
     for copy in last:
@@ -253,7 +277,8 @@
                         pltpu.VMEM((devices, SUB, LANES), bf16),
                         pltpu.VMEM((devices - 1, SUB, LANES), bf16),
                         dma((2,)), dma((2,)), dma((2, YS - 1)), dma((2, YS - 1)),
-                        dma((devices - 1,)), dma((devices - 1,))],
+                        dma((devices - 1,)), dma((devices - 1,)),
+                        pltpu.SemaphoreType.REGULAR((3,))],
         compiler_params=pltpu.CompilerParams(collective_id=0, has_side_effects=True),
         name="stack",
     )(moveout, active, seismic[0], templates[0].transpose(1, 0, 2))

time: 40.1 us -> 37.3 us (0.930)
  Pallas kernels: 38.6 us -> 35.8 us
    pallas_call x1, Pallas kernels: 38.6 us -> 35.8 us  [per_device(): pl.pallas_call(stack_kernel, out_shape=jax.ShapeDtypeStruct((SUB, LANES),...]
where the time goes in v4:
time: 37.3 us; the launch traced here: 37.1 us
  Pallas kernels  35.8 us (96%)
  local copies, waits for them, and re-layouts  1.28 us (3%)
    pallas_call x1, Pallas kernels, per_device(): pl.pallas_call(stack_kernel, out_shape=jax.ShapeDtypeStruct((SUB, LANES),...  35.8 us
    unnamed x1, local copies, waits for them, and re-layouts  1.28 us

profile of v4, /device:TPU:1, one launch (start us, length us, event | category | flops | bytes accessed | tf_op | source)
XLA Modules:
  0.0 37.1 jit_solution(16641168049991054920)
XLA Ops:
  0.0 35.8 %stack.1 = f32[8,128]{1,0:T(8,128)} custom-call(s32[16,32]{1,0:T(8,128)} %shift_ref.1, s32[16]{0:T(128)} %active_ref.1, bf16[3,16384]{1,0:T(4,128)(2,1)} %bitcast.5, bf16[3,32,256]{2,1,0:T(8,128)(2,1)} %bitcast.6), custom_call_target="tpu_custom_call" | custom-call | tf_op jit(solution)/shard_map/stack/pallas_call | solution.py:258
  35.9 1.3 %copy.6 = f32[1,1024]{1,0:T(1,128)} copy(f32[1,1024]{1,0:T(1,128)} %bitcast.7) | data formatting | bytes 8192

commit v5 on v4

--- a/solution.py
+++ b/solution.py
@@ -28,8 +28,8 @@
     return tile
 
 
-def stack_kernel(shift_ref, active_ref, seis_ref, wave_ref, out_ref,
-                 xs_ref, tg_ref, gs, gr, gl, rows_ref, moved_ref, w_ref, f_ref, acc_ref,
+def stack_kernel(shift_hbm, active_hbm, seis_ref, wave_ref, out_ref,
+                 shift_ref, active_ref, xs_ref, tg_ref, gs, gr, gl, rows_ref, moved_ref, w_ref, f_ref, acc_ref,
                  core_send, core_recv, sum_ref, y_send, y_recv, plane_ref, z_send, z_recv,
                  s1, r1, s2, r2, s3, r3, ready):
     tm, tmpl = lax.axis_index("tm"), lax.axis_index("tmpl")
@@ -80,13 +80,13 @@
     for target in targets:
         pl.semaphore_signal(barrier, inc=1, device_id=target, device_id_type=MESH)
 
-    local = [pltpu.make_async_copy(wave_ref, tg_ref.at[x], gl.at[0])]
+    local = [pltpu.make_async_copy(wave_ref, tg_ref.at[x], gl.at[0]),
+             pltpu.make_async_copy(shift_hbm, shift_ref, gl.at[3]),
+             pltpu.make_async_copy(active_hbm, active_ref, gl.at[4])]
     local += [pltpu.make_async_copy(*pair, gl.at[1 + k]) for k, pair in enumerate(pieces(x))]
     for copy in local:
         copy.start()
     acc_ref[...] = jnp.zeros_like(acc_ref)
-    for copy in local:
-        copy.wait()
     nrows = xs_ref.shape[2] // LANES
 
     def multiply(s, c, part):
@@ -155,19 +155,24 @@
             to_y(part, d, py).start()
 
     gather = []
-    for d in (1, 3):
-        gather.append(send(0, wave_ref, tg_ref.at[x], d, XS - d))
-    for d in (1, 3, 2):
+    for c in range(CH):
+        for d in (3, 1):
+            gather.append(send(c, wave_ref.at[c], tg_ref.at[x, c], d, XS - d))
+    for d in (3, 1, 2):
         for k, (source, target) in enumerate(pieces((x + d) % XS)):
-            gather.append(send(1 + k, source, target, d, XS - d))
-    onward = tg_ref.at[(x + 1) % XS]
-    relay = pltpu.make_async_remote_copy(
-        src_ref=onward, dst_ref=onward, send_sem=gs.at[0, 2], recv_sem=gr.at[0, 2],
-        device_id=along_x((x + 3) % XS), device_id_type=MESH)
+            gather.append(send(CH + k, source, target, d, XS - d))
+    relay = []
+    for c in range(CH):
+        onward = tg_ref.at[(x + 1) % XS, c]
+        relay.append(pltpu.make_async_remote_copy(
+            src_ref=onward, dst_ref=onward, send_sem=gs.at[c, 2], recv_sem=gr.at[c, 2],
+            device_id=along_x((x + 3) % XS), device_id_type=MESH))
     pl.semaphore_wait(barrier, len(targets))
     for copy in gather:
         copy.start()
     tell(1)
+    for copy in local:
+        copy.wait()
 
     def arrive(step, carry):
         offset = step ^ (step // 2)
@@ -175,15 +180,16 @@
 
         @pl.when(step > 0)
         def _():
-            send(0, wave_ref, tg_ref.at[s], 1, offset).wait_recv()
-
-            @pl.when(step == 1)
-            def _():
-                relay.start()
+            for c in range(CH):
+                send(c, wave_ref.at[c], tg_ref.at[s, c], 1, offset).wait_recv()
+
+                @pl.when(step == 1)
+                def _():
+                    relay[c].start()
 
             for k, (source, _) in enumerate(pieces(x)):
                 target = xs_ref.at[s, :, k * quarter : k * quarter + source.shape[1]]
-                send(1 + k, source, target, 1, offset).wait_recv()
+                send(CH + k, source, target, 1, offset).wait_recv()
 
         @pl.when(step == 1)
         def _():
@@ -211,9 +217,15 @@
     to_core(1).start()
     after_core(0)
     after_core(1)
-    for copy in gather + [relay]:
+    for copy in gather + relay:
         copy.wait_send()
 
+    last = [
+        pltpu.make_async_remote_copy(
+            src_ref=z_send.at[pz], dst_ref=z_recv.at[d], send_sem=s3.at[d], recv_sem=r3.at[d],
+            device_id=place(y, pz, core), device_id_type=MESH)
+        for d, pz in zs]
+    heard(4)
     for part in range(2):
         total = sum_ref[part, pl.ds(pl.multiple_of(y * block, block), block)]
         for d, py in ys:
@@ -225,25 +237,15 @@
                 at = (2 * part + k) * ZL + pzl
                 plane_ref[at] = tile
                 z_send[at] = tile.astype(jnp.bfloat16)
-
-    last = [
-        pltpu.make_async_remote_copy(
-            src_ref=z_send.at[pz], dst_ref=z_recv.at[d], send_sem=s3.at[d], recv_sem=r3.at[d],
-            device_id=place(y, pz, core), device_id_type=MESH)
-        for d, pz in zs]
-    heard(4)
-    for copy in last:
-        copy.start()
+        for copy, (_, pz) in zip(last, zs):
+            pl.when(pz // (nz // 2) == part)(copy.start)
+
     for copy in last:
         copy.wait()
     total = plane_ref[z]
     for d in range(nz - 1):
         total = total + z_recv[d].astype(jnp.float32)
     out_ref[...] = transpose_groups(total)
-
-
-def vmem(count):
-    return [pl.BlockSpec(memory_space=pltpu.VMEM)] * count
 
 
 def per_device(seismic, templates, moveout, active):
@@ -258,11 +260,13 @@
     tile = pl.pallas_call(
         stack_kernel,
         out_shape=jax.ShapeDtypeStruct((SUB, LANES), f32),
-        in_specs=[pl.BlockSpec(memory_space=pltpu.SMEM)] * 2 + vmem(2),
-        out_specs=vmem(1)[0],
-        scratch_shapes=[pltpu.VMEM((XS, CH, span), bf16),
+        in_specs=[pl.BlockSpec(memory_space=pl.ANY)] * 4,
+        out_specs=pl.BlockSpec(memory_space=pltpu.VMEM),
+        scratch_shapes=[pltpu.SMEM(moveout.shape, moveout.dtype),
+                        pltpu.SMEM(active.shape, active.dtype),
+                        pltpu.VMEM((XS, CH, span), bf16),
                         pltpu.VMEM((XS, CH, TPL, L), bf16),
-                        dma((3, XS)), dma((3, XS)), dma((3,)),
+                        dma((CH + 2, XS)), dma((CH + 2, XS)), dma((5,)),
                         pltpu.VMEM((XS, CH, 40, LANES), f32),
                         pltpu.VMEM((TPL, SUB, NF), f32),
                         pltpu.VMEM((XS, CH, rows, NF), bf16),

time: 37.3 us -> 35.9 us (0.962)
  Pallas kernels: 35.8 us -> 34.1 us
    pallas_call x1, Pallas kernels: 35.8 us -> 34.1 us  [per_device(): pl.pallas_call(stack_kernel, out_shape=jax.ShapeDtypeStruct((SUB, LANES),...]
where the time goes in v5:
time: 35.9 us; the launch traced here: 35.4 us
  Pallas kernels  34.1 us (95%)
  local copies, waits for them, and re-layouts  1.28 us (4%)
    pallas_call x1, Pallas kernels, per_device(): pl.pallas_call(stack_kernel, out_shape=jax.ShapeDtypeStruct((SUB, LANES),...  34.1 us
    unnamed x1, local copies, waits for them, and re-layouts  1.28 us

profile of v5, /device:TPU:1, one launch (start us, length us, event | category | flops | bytes accessed | tf_op | source)
XLA Modules:
  0.0 35.4 jit_solution(10651470332414235823)
XLA Ops:
  0.0 34.1 %stack.1 = f32[8,128]{1,0:T(8,128)} custom-call(s32[16,32]{1,0:T(8,128)} %shift_hbm.1, s32[16]{0:T(128)} %active_hbm.1, bf16[3,16384]{1,0:T(4,128)(2,1)} %bitcast.5, bf16[3,32,256]{2,1,0:T(8,128)(2,1)} %bitcast.6), custom_call_target="tpu_custom_call" | custom-call | tf_op jit(solution)/shard_map/stack/pallas_call | solution.py:260
  34.1 1.3 %copy.6 = f32[1,1024]{1,0:T(1,128)} copy(f32[1,1024]{1,0:T(1,128)} %bitcast.7) | data formatting | bytes 8192

commit v6 on v5

--- a/solution.py
+++ b/solution.py
@@ -89,21 +89,7 @@
     acc_ref[...] = jnp.zeros_like(acc_ref)
     nrows = xs_ref.shape[2] // LANES
 
-    def multiply(s, c, part):
-        frames = jnp.concatenate(
-            [rows_ref[s, c, u + 16 * part : u + 16 * part + 16, :] for u in range(NF // BLK)], axis=1)
-        for j in range(0, 16, 2):
-            even = frames if j == 0 else pltpu.roll(frames, NF - SUB * j, 1)
-            odd = pltpu.roll(frames, NF - SUB * (j + 1), 1)
-            for k in range(2):
-                top = k * LANES + SUB * j
-                both = jnp.concatenate(
-                    [even[SUB * k : SUB * k + SUB], odd[SUB * k : SUB * k + SUB]], axis=0)
-                f_ref[top : top + 2 * SUB, :] = both.astype(jnp.bfloat16)
-        acc_ref[part] += lax.dot_general(
-            w_ref[s, c], f_ref[...], (((1,), (1,)), ((), ())), preferred_element_type=jnp.float32)
-
-    def early(s):
+    def sample_frames(s):
         scale = active_ref[s * ZH + zh].astype(jnp.float32)
         column = lax.broadcasted_iota(jnp.int32, xs_ref.shape[1:], 1)
         last_quarter = jnp.full(xs_ref.shape[1:], x, jnp.int32) == XS - 1
@@ -111,7 +97,19 @@
         signal = jnp.where(past, 0.0, xs_ref[s].astype(jnp.float32) * scale)
         for c in range(CH):
             for r in range(nrows):
-                rows_ref[s, c, r : r + 1, :] = signal[c : c + 1, r * LANES : (r + 1) * LANES]
+                rows_ref[c, r : r + 1, :] = signal[c : c + 1, r * LANES : (r + 1) * LANES]
+        for c in range(CH):
+            frames = jnp.concatenate([rows_ref[c, u : u + 32, :] for u in range(NF // BLK)], axis=1)
+            for j in range(0, 16, 2):
+                even = frames if j == 0 else pltpu.roll(frames, NF - SUB * j, 1)
+                odd = pltpu.roll(frames, NF - SUB * (j + 1), 1)
+                for k in range(ZH):
+                    top = k % 2 * LANES + SUB * j
+                    both = jnp.concatenate(
+                        [even[SUB * k : SUB * k + SUB], odd[SUB * k : SUB * k + SUB]], axis=0)
+                    f_ref[c, k // 2, top : top + 2 * SUB, :] = both.astype(jnp.bfloat16)
+
+    def template_rows(s):
         waves = [tg_ref[s, c].astype(jnp.float32) for c in range(CH)]
         for t in range(TPL):
             wave = jnp.concatenate([w[t : t + 1] for w in waves], axis=0)
@@ -124,13 +122,14 @@
                     t = (slot % 16) * 2 + slot // 16
                     wide = jnp.broadcast_to(moved_ref[t, c : c + 1, :], (SUB, NF))
                     pair.append(pltpu.roll(wide, 0, 1, stride=1, stride_axis=0))
-                w_ref[s, c, at * SUB : (at + 2) * SUB, :] = jnp.concatenate(
+                w_ref[c, at * SUB : (at + 2) * SUB, :] = jnp.concatenate(
                     pair, axis=0).astype(jnp.bfloat16)
-            multiply(s, c, 0)
-
-    def late(s):
+
+    def multiply(part):
         for c in range(CH):
-            multiply(s, c, 1)
+            acc_ref[part] += lax.dot_general(
+                w_ref[c], f_ref[c, part], (((1,), (1,)), ((), ())),
+                preferred_element_type=jnp.float32)
 
     away = pl.ds(pl.multiple_of((1 - core) * half, SUB), half)
     mine = pl.ds(pl.multiple_of(core * half, SUB), half)
@@ -178,15 +177,17 @@
         offset = step ^ (step // 2)
         s = (x + offset) % XS
 
+        def templates_here(c):
+            send(c, wave_ref.at[c], tg_ref.at[s, c], 1, offset).wait_recv()
+
+        @pl.when(step == 1)
+        def _():
+            for c in range(CH):
+                templates_here(c)
+                relay[c].start()
+
         @pl.when(step > 0)
         def _():
-            for c in range(CH):
-                send(c, wave_ref.at[c], tg_ref.at[s, c], 1, offset).wait_recv()
-
-                @pl.when(step == 1)
-                def _():
-                    relay[c].start()
-
             for k, (source, _) in enumerate(pieces(x)):
                 target = xs_ref.at[s, :, k * quarter : k * quarter + source.shape[1]]
                 send(CH + k, source, target, 1, offset).wait_recv()
@@ -201,18 +202,26 @@
             heard(2)
             tell(4)
 
-        early(s)
+        sample_frames(s)
+
+        @pl.when(step > 1)
+        def _():
+            for c in range(CH):
+                templates_here(c)
+
+        template_rows(s)
+        multiply(0)
 
         @pl.when(step < XS - 1)
         def _():
-            late(s)
+            multiply(1)
 
         return carry
 
     lax.fori_loop(0, XS, arrive, 0)
     core_send[0] = acc_ref[0, away].astype(jnp.bfloat16)
     to_core(0).start()
-    late((x + 2) % XS)
+    multiply(1)
     core_send[1] = acc_ref[1, away].astype(jnp.bfloat16)
     to_core(1).start()
     after_core(0)
@@ -267,10 +276,10 @@
                         pltpu.VMEM((XS, CH, span), bf16),
                         pltpu.VMEM((XS, CH, TPL, L), bf16),
                         dma((CH + 2, XS)), dma((CH + 2, XS)), dma((5,)),
-                        pltpu.VMEM((XS, CH, 40, LANES), f32),
+                        pltpu.VMEM((CH, 40, LANES), f32),
                         pltpu.VMEM((TPL, SUB, NF), f32),
-                        pltpu.VMEM((XS, CH, rows, NF), bf16),
-                        pltpu.VMEM((columns, NF), bf16),
+                        pltpu.VMEM((CH, rows, NF), bf16),
+                        pltpu.VMEM((CH, 2, columns, NF), bf16),
                         pltpu.VMEM((2, rows, columns), f32),
                         pltpu.VMEM((2, half, columns), bf16),
                         pltpu.VMEM((2, half, columns), bf16),

time: 35.9 us -> 36.7 us (1.022)
  the two profiles are of different devices: /device:TPU:1 before, /device:TPU:6 now
where the time goes in v6:
time: 36.7 us; the launch traced here: 36.5 us
  Pallas kernels  35.2 us (96%)
  local copies, waits for them, and re-layouts  1.28 us (3%)
    pallas_call x1, Pallas kernels, per_device(): pl.pallas_call(stack_kernel, out_shape=jax.ShapeDtypeStruct((SUB, LANES),...  35.2 us
    unnamed x1, local copies, waits for them, and re-layouts  1.28 us

profile of v6, /device:TPU:6, one launch (start us, length us, event | category | flops | bytes accessed | tf_op | source)
XLA Modules:
  0.0 36.5 jit_solution(8778222931078390873)
XLA Ops:
  0.0 35.2 %stack.1 = f32[8,128]{1,0:T(8,128)} custom-call(s32[16,32]{1,0:T(8,128)} %shift_hbm.1, s32[16]{0:T(128)} %active_hbm.1, bf16[3,16384]{1,0:T(4,128)(2,1)} %bitcast.5, bf16[3,32,256]{2,1,0:T(8,128)(2,1)} %bitcast.6), custom_call_target="tpu_custom_call" | custom-call | tf_op jit(solution)/shard_map/stack/pallas_call | solution.py:269
  35.2 1.3 %copy.6 = f32[1,1024]{1,0:T(1,128)} copy(f32[1,1024]{1,0:T(1,128)} %bitcast.7) | data formatting | bytes 8192

commit v7 on v5

--- a/solution.py
+++ b/solution.py
@@ -155,12 +155,19 @@
             to_y(part, d, py).start()
 
     gather = []
-    for c in range(CH):
-        for d in (3, 1):
-            gather.append(send(c, wave_ref.at[c], tg_ref.at[x, c], d, XS - d))
-    for d in (3, 1, 2):
+    def samples(d):
         for k, (source, target) in enumerate(pieces((x + d) % XS)):
             gather.append(send(CH + k, source, target, d, XS - d))
+
+    def waveforms(d):
+        for c in range(CH):
+            gather.append(send(c, wave_ref.at[c], tg_ref.at[x, c], d, XS - d))
+
+    waveforms(3)
+    samples(2)
+    waveforms(1)
+    samples(3)
+    samples(1)
     relay = []
     for c in range(CH):
         onward = tg_ref.at[(x + 1) % XS, c]

time: 35.9 us -> 36.4 us (1.014)
  Pallas kernels: 34.1 us -> 34.5 us
    pallas_call x1, Pallas kernels: 34.1 us -> 34.5 us  [per_device(): pl.pallas_call(stack_kernel, out_shape=jax.ShapeDtypeStruct((SUB, LANES),...]
where the time goes in v7:
time: 36.4 us; the launch traced here: 35.8 us
  Pallas kernels  34.5 us (95%)
  local copies, waits for them, and re-layouts  1.28 us (4%)
    pallas_call x1, Pallas kernels, per_device(): pl.pallas_call(stack_kernel, out_shape=jax.ShapeDtypeStruct((SUB, LANES),...  34.5 us
    unnamed x1, local copies, waits for them, and re-layouts  1.28 us

profile of v7, /device:TPU:1, one launch (start us, length us, event | category | flops | bytes accessed | tf_op | source)
XLA Modules:
  0.0 35.8 jit_solution(14154682286116066804)
XLA Ops:
  0.0 34.5 %stack.1 = f32[8,128]{1,0:T(8,128)} custom-call(s32[16,32]{1,0:T(8,128)} %shift_hbm.1, s32[16]{0:T(128)} %active_hbm.1, bf16[3,16384]{1,0:T(4,128)(2,1)} %bitcast.5, bf16[3,32,256]{2,1,0:T(8,128)(2,1)} %bitcast.6), custom_call_target="tpu_custom_call" | custom-call | tf_op jit(solution)/shard_map/stack/pallas_call | solution.py:267
  34.5 1.3 %copy.6 = f32[1,1024]{1,0:T(1,128)} copy(f32[1,1024]{1,0:T(1,128)} %bitcast.7) | data formatting | bytes 8192

commit v8 on v5

--- a/solution.py
+++ b/solution.py
@@ -156,17 +156,11 @@
 
     gather = []
     for c in range(CH):
-        for d in (3, 1):
+        for d in (2, 3, 1):
             gather.append(send(c, wave_ref.at[c], tg_ref.at[x, c], d, XS - d))
     for d in (3, 1, 2):
         for k, (source, target) in enumerate(pieces((x + d) % XS)):
             gather.append(send(CH + k, source, target, d, XS - d))
-    relay = []
-    for c in range(CH):
-        onward = tg_ref.at[(x + 1) % XS, c]
-        relay.append(pltpu.make_async_remote_copy(
-            src_ref=onward, dst_ref=onward, send_sem=gs.at[c, 2], recv_sem=gr.at[c, 2],
-            device_id=along_x((x + 3) % XS), device_id_type=MESH))
     pl.semaphore_wait(barrier, len(targets))
     for copy in gather:
         copy.start()
@@ -182,10 +176,6 @@
         def _():
             for c in range(CH):
                 send(c, wave_ref.at[c], tg_ref.at[s, c], 1, offset).wait_recv()
-
-                @pl.when(step == 1)
-                def _():
-                    relay[c].start()
 
             for k, (source, _) in enumerate(pieces(x)):
                 target = xs_ref.at[s, :, k * quarter : k * quarter + source.shape[1]]
@@ -217,7 +207,7 @@
     to_core(1).start()
     after_core(0)
     after_core(1)
-    for copy in gather + relay:
+    for copy in gather:
         copy.wait_send()
 
     last = [

time: 35.9 us -> 36.4 us (1.014)
  Pallas kernels: 34.1 us -> 34.6 us
    pallas_call x1, Pallas kernels: 34.1 us -> 34.6 us  [per_device(): pl.pallas_call(stack_kernel, out_shape=jax.ShapeDtypeStruct((SUB, LANES),...]
where the time goes in v8:
time: 36.4 us; the launch traced here: 35.9 us
  Pallas kernels  34.6 us (95%)
  local copies, waits for them, and re-layouts  1.28 us (4%)
    pallas_call x1, Pallas kernels, per_device(): pl.pallas_call(stack_kernel, out_shape=jax.ShapeDtypeStruct((SUB, LANES),...  34.6 us
    unnamed x1, local copies, waits for them, and re-layouts  1.28 us

profile of v8, /device:TPU:1, one launch (start us, length us, event | category | flops | bytes accessed | tf_op | source)
XLA Modules:
  0.0 35.9 jit_solution(5295827007461819514)
XLA Ops:
  0.0 34.6 %stack.1 = f32[8,128]{1,0:T(8,128)} custom-call(s32[16,32]{1,0:T(8,128)} %shift_hbm.1, s32[16]{0:T(128)} %active_hbm.1, bf16[3,16384]{1,0:T(4,128)(2,1)} %bitcast.5, bf16[3,32,256]{2,1,0:T(8,128)(2,1)} %bitcast.6), custom_call_target="tpu_custom_call" | custom-call | tf_op jit(solution)/shard_map/stack/pallas_call | solution.py:250
  34.6 1.3 %copy.6 = f32[1,1024]{1,0:T(1,128)} copy(f32[1,1024]{1,0:T(1,128)} %bitcast.7) | data formatting | bytes 8192
